TPU v7x, 32 devices: a whole 2x2x4 slice. The times are simulated.
32 devices in a mesh: groups: 2 (over y), hist: 2 (over x), rows: 4 (over z), cols: 2 (over core).
Axes of the slice: x: 2, y: 2, z: 4, core: 2. Of those that a mesh axis runs over, the one named last changes fastest.
Arguments:
- hists: float32 [2, 1024, 4096], P('hist', ('groups', 'rows'), 'cols'), parts along dimension 1, may hold values from 0.2 to 2000, as said below
- log_scaling_fields: float32 [2, 1024, 4096], P('hist', ('groups', 'rows'), 'cols'), parts along dimension 1, may hold values from -1 to 1
- histogram_weight_list: float32 [2], replicated, may hold values from 0.25 to 4
Outputs:
- barycenter: float32 [1024, 4096], P(('groups', 'rows'), 'cols'), parts along dimension 0
- new_logs: float32 [2, 1024, 4096], P('hist', ('groups', 'rows'), 'cols'), parts along dimension 1
There are 2 independent parts, one for each index of `groups`. A program takes and returns all parts, laid end to end along the dimension named above; an argument that names none is the same for every part. Nothing has to cross between parts.
Inputs may be any that keep to these rules, and one draw needn't show every extreme that they name: `hists`: every entry is positive.
All inputs are finite; a program needn't handle non-finite values.
Results may differ from a plain program's by a relative error of at most 0.00021.
Values sent between devices are 32-bit elements; how exact they have to be, the bound alone decides.
A program may use at most 64 MiB of HBM per device.

v0:
```python
import jax
import jax.numpy as jnp
from jax import lax
from jax.sharding import PartitionSpec as P

HALF = 32


kernel_sigma = 16.0


def padded_2(cells, sides, width):
    for axis, dim in sides:
        count = lax.axis_size(axis)
        ends = count - 1
        head = lax.slice_in_dim(cells, 0, width, axis=dim)
        tail = lax.slice_in_dim(cells, cells.shape[dim] - width, cells.shape[dim], axis=dim)
        cells = jnp.concatenate(
            [
                lax.ppermute(tail, axis, [(i, (i + 1) % count) for i in range(ends)]),
                cells,
                lax.ppermute(head, axis, [((i + 1) % count, i) for i in range(ends)]),
            ],
            axis=dim,
        )
    return cells


def band_matrix(width_out):
    shape_full = (width_out + 2 * HALF, width_out)
    rows_in = lax.broadcasted_iota(jnp.int32, shape_full, 0)
    cols_out = lax.broadcasted_iota(jnp.int32, shape_full, 1)
    offsets = (rows_in - cols_out - HALF).astype(jnp.float32)
    tap_offsets = jnp.arange(-HALF, HALF + 1).astype(jnp.float32)
    tap_total = jnp.sum(jnp.exp(-tap_offsets * tap_offsets / (2.0 * kernel_sigma * kernel_sigma)))
    entries = jnp.exp(-offsets * offsets / (2.0 * kernel_sigma * kernel_sigma)) / tap_total
    return jnp.where(jnp.abs(offsets) <= HALF, entries, 0.0)


def column_pass(padded, width_out):
    block_list = []
    for offset in range(0, width_out, 256):
        span_cols = min(256, width_out - offset)
        window = padded[:, offset : offset + span_cols + 2 * HALF]
        block_list.append(
            jnp.dot(
                window,
                band_matrix(span_cols),
                precision=lax.Precision.HIGHEST,
                preferred_element_type=jnp.float32,
            )
        )
    return jnp.concatenate(block_list, axis=1)


def row_pass(across, height_out):
    return jnp.dot(
        band_matrix(height_out).T,
        across,
        precision=lax.Precision.HIGHEST,
        preferred_element_type=jnp.float32,
    )


def blurred_patch(padded, height_out, width_out):
    return row_pass(column_pass(padded, width_out), height_out)


def neighbor_total(values):
    return padded_2(values, (("rows", 0), ("cols", 1)), HALF)


def body(hists, log_scaling_fields, histogram_weight_list):
    masses = hists[0]
    local_log_values = log_scaling_fields[0]
    patch_height = masses.shape[0]
    patch_width = masses.shape[1]
    scaling_fields = jnp.exp(local_log_values)
    blurred_vertical = blurred_patch(neighbor_total(scaling_fields), patch_height, patch_width)
    ratios = masses / blurred_vertical
    smooth_u = blurred_patch(neighbor_total(ratios), patch_height, patch_width)
    log_blurred = jnp.log(smooth_u)
    log_portions = local_log_values + log_blurred
    position = lax.axis_index("hist")
    own_pick = lax.broadcasted_iota(jnp.int32, histogram_weight_list.shape, 0) == position
    own_weight = jnp.sum(jnp.where(own_pick, histogram_weight_list, 0.0)) / jnp.sum(
        histogram_weight_list
    )
    weighted = own_weight * log_portions
    cell_count = patch_height * lax.axis_size("rows") * patch_width * lax.axis_size("cols")
    log_mean = lax.psum(weighted, "hist")
    mean_field = jnp.exp(log_mean)
    total_mass = lax.psum(jnp.sum(mean_field), ("rows", "cols"))
    barycenter = mean_field * (cell_count / total_mass)
    new_logs = jnp.log(barycenter) - log_blurred
    return (barycenter, new_logs[None])


def solution(mesh):
    return jax.shard_map(
        body,
        mesh=mesh,
        in_specs=(
            P("hist", ("groups", "rows"), "cols"),
            P("hist", ("groups", "rows"), "cols"),
            P(),
        ),
        out_specs=(P(("groups", "rows"), "cols"), P("hist", ("groups", "rows"), "cols")),
        check_vma=False,
    )
```

profile of v0, /device:TPU:0, one launch (start us, length us, event | category | flops | bytes accessed | tf_op | source)
XLA Modules:
  0.0 137.3 jit_solution(3415353745641295112)
XLA Ops:
  7.2 0.0 all-reduce.2.cloned.1.call-start
  7.2 1.4 %bitcast_exponential_fusion = f32[128,2048]{1,0:T(8,128)S(1)} fusion(f32[1,128,2048]{2,1,0:T(8,128)} %param.4), kind=kLoop, calls=%fused_computation.21 | loop fusion | bytes 2097152 | tf_op jit(solution)/shard_map/exp | solution.py:78
  8.6 5.0 %collective-permute-start = (f32[32,2048]{1,0:T(8,128)S(1)}, f32[32,2048]{1,0:T(8,128)S(1)}, u32[]{:S(2)}, u32[]{:S(2)}) collective-permute-start(f32[32,2048]{1,0:T(8,128)S(1)} %get-tuple-element.12), channel_id=1, source_target_pairs={{0,2},{2,4},{4,6},{1,3},{3,5},{5,7},{8,10},{10,12},{12,14},{9,11},... | collective-permute-start | bytes 786440 | tf_op jit(solution)/shard_map/ppermute | solution.py:20
  13.6 1.3 collective-permute-start.1
  14.9 0.6 fusion.45
  15.6 3.6 %collective-permute-done = f32[32,2048]{1,0:T(8,128)S(1)} collective-permute-done((f32[32,2048]{1,0:T(8,128)S(1)}, f32[32,2048]{1,0:T(8,128)S(1)}, u32[]{:S(2)}, u32[]{:S(2)}) %collective-permute-start) | collective-permute-done | bytes 262176 | tf_op jit(solution)/shard_map/ppermute | solution.py:20
  19.2 4.1 %collective-permute-done.1 = f32[32,2048]{1,0:T(8,128)S(1)} collective-permute-done((f32[32,2048]{1,0:T(8,128)S(1)}, f32[32,2048]{1,0:T(8,128)S(1)}, u32[]{:S(2)}, u32[]{:S(2)}) %collective-permute-start.1) | collective-permute-done | bytes 262176 | tf_op jit(solution)/shard_map/ppermute | solution.py:22
  23.3 0.1 pad_maximum_fusion.28
  23.4 1.3 collective-permute-start.2
  24.7 1.3 collective-permute-start.3
  26.0 0.1 pad_maximum_fusion
  26.1 0.0 collective-permute-done.2
  26.1 1.2 convolution_dynamic-update-slice_fusion.15
  27.4 1.2 convolution_dynamic-update-slice_fusion.14
  28.6 1.2 convolution_dynamic-update-slice_fusion.13
  29.9 1.2 convolution_dynamic-update-slice_fusion.12
  31.1 1.2 convolution_dynamic-update-slice_fusion.11
  32.3 1.2 convolution_dynamic-update-slice_fusion.10
  33.6 1.2 convolution_dynamic-update-slice_fusion.9
  34.8 0.0 copy-start.3
  34.8 0.0 collective-permute-done.3
  34.8 1.3 convolution_dynamic-update-slice_fusion.8
  36.2 0.0 copy-done.3
  36.2 0.0 copy-start.2
  36.2 1.8 %convolution_divide_fusion = f32[128,2048]{1,0:T(8,128)S(1)} fusion(f32[192,2048]{1,0:T(8,128)S(1)} %convolution_dynamic-update-slice_fusion.8, f32[1,128,2048]{2,1,0:T(8,128)S(1)} %copy-done.3, f32[]{:T(128)} %fusion.45), kind=kOutput, calls=%fused_computation.1 | convolution fusion | flops 604487680 | bytes 3670020 | tf_op jit(solution)/shard_map/dot_general | solution.py:57
  38.0 3.5 %collective-permute-start.4 = (f32[32,2048]{1,0:T(8,128)S(1)}, f32[32,2048]{1,0:T(8,128)S(1)}, u32[]{:S(2)}, u32[]{:S(2)}) collective-permute-start(f32[32,2048]{1,0:T(8,128)S(1)} %get-tuple-element.10), channel_id=1, source_target_pairs={{0,2},{2,4},{4,6},{1,3},{3,5},{5,7},{8,10},{10,12},{12,14},{9,11},... | collective-permute-start | bytes 786440 | tf_op jit(solution)/shard_map/ppermute | solution.py:20
  41.5 1.3 collective-permute-start.5
  42.8 0.0 copy-done.2
  42.8 0.6 fusion.123
  44.8 3.2 %collective-permute-done.4 = f32[32,2048]{1,0:T(8,128)S(1)} collective-permute-done((f32[32,2048]{1,0:T(8,128)S(1)}, f32[32,2048]{1,0:T(8,128)S(1)}, u32[]{:S(2)}, u32[]{:S(2)}) %collective-permute-start.4) | collective-permute-done | bytes 262176 | tf_op jit(solution)/shard_map/ppermute | solution.py:20
  48.0 4.5 %collective-permute-done.5 = f32[32,2048]{1,0:T(8,128)S(1)} collective-permute-done((f32[32,2048]{1,0:T(8,128)S(1)}, f32[32,2048]{1,0:T(8,128)S(1)}, u32[]{:S(2)}, u32[]{:S(2)}) %collective-permute-start.5) | collective-permute-done | bytes 262176 | tf_op jit(solution)/shard_map/ppermute | solution.py:22
  52.5 0.1 pad_maximum_fusion.26
  52.6 1.9 %collective-permute-start.6 = (f32[192,32]{1,0:T(8,128)S(1)}, f32[192,32]{1,0:T(8,128)S(1)}, u32[]{:S(2)}, u32[]{:S(2)}) collective-permute-start(f32[192,32]{1,0:T(8,128)S(1)} %get-tuple-element.7), channel_id=1, source_target_pairs={{0,1},{2,3},{4,5},{6,7},{8,9},{10,11},{12,13},{14,15},{16,17},{18,... | collective-permute-start | bytes 73736 | tf_op jit(solution)/shard_map/ppermute | solution.py:20
  54.5 1.5 %collective-permute-start.7 = (f32[192,32]{1,0:T(8,128)S(1)}, f32[192,32]{1,0:T(8,128)S(1)}, u32[]{:S(2)}, u32[]{:S(2)}) collective-permute-start(f32[192,32]{1,0:T(8,128)S(1)} %get-tuple-element.6), channel_id=1, source_target_pairs={{1,0},{3,2},{5,4},{7,6},{9,8},{11,10},{13,12},{15,14},{17,16},{19,... | collective-permute-start | bytes 73736 | tf_op jit(solution)/shard_map/ppermute | solution.py:22
  55.9 0.1 pad_maximum_fusion.1
  56.1 0.0 collective-permute-done.6
  56.1 1.2 convolution_dynamic-update-slice_fusion.7
  57.3 1.2 convolution_dynamic-update-slice_fusion.6
  58.5 1.2 convolution_dynamic-update-slice_fusion.5
  59.8 1.2 convolution_dynamic-update-slice_fusion.4
  61.0 1.2 convolution_dynamic-update-slice_fusion.3
  62.3 1.2 convolution_dynamic-update-slice_fusion.2
  63.5 1.2 convolution_dynamic-update-slice_fusion.1
  64.7 0.0 copy-start
  64.7 0.0 collective-permute-done.7
  64.8 1.3 convolution_dynamic-update-slice_fusion
  66.1 0.0 copy-done
  66.1 2.8 %fusion = (f32[128,2048]{1,0:T(8,128)}, f32[128,2048]{1,0:T(8,128)S(1)}) fusion(f32[1,128,2048]{2,1,0:T(8,128)S(1)} %copy-done, f32[]{:T(128)S(6)} %div.20, f32[192,2048]{1,0:T(8,128)S(1)} %convolution_dynamic-update-slice_fusion, f32[]{:T(128)} %fusion.45), kind=kOutput, calls=%fused_computation.22 | convolution fusion | flops 604749824 | bytes 4718600 | tf_op jit(solution)/shard_map/dot_general | solution.py:57
  68.9 0.0 all-reduce.2.cloned.1.call-update
  69.0 40.2 %all-reduce.2.cloned.1.call-done = f32[128,2048]{1,0:T(8,128)} async-done(((f32[128,2048]{1,0:T(8,128)}), f32[128,2048]{1,0:T(8,128)}) %all-reduce.2.cloned.1.call-update) | async-done | bytes 1048592 | tf_op jit(solution)/shard_map/psum | solution.py:91
  109.2 0.0 copy-start.1
  109.2 2.2 %exponential_reduce_fusion = f32[]{:T(128)} fusion(f32[128,2048]{1,0:T(8,128)} %all-reduce.2.cloned.1.call-done), kind=kLoop, calls=%fused_computation.25 | loop fusion | flops 262143 | bytes 1048580 | tf_op jit(solution)/shard_map/reduce_sum | solution.py:93
  111.4 16.8 %psum.15 = f32[]{:T(128)} all-reduce(f32[]{:T(128)} %exponential_reduce_fusion), channel_id=1, replica_groups=mesh['groups'=2,'hist'=2,'rows'=4,'cols'=2] {'rows','cols'}, use_global_device_ids=true, to_apply=%region_5.6 | all-reduce | flops 1 | bytes 8 | tf_op jit(solution)/shard_map/psum | solution.py:93
  128.9 0.0 copy-done.1
  128.9 1.6 %subtract_bitcast_fusion = (f32[1,128,2048]{2,1,0:T(8,128)}, f32[128,2048]{1,0:T(8,128)}) fusion(f32[128,2048]{1,0:T(8,128)S(1)} %get-tuple-element.15, f32[]{:T(128)S(6)} %div.29, f32[128,2048]{1,0:T(8,128)S(1)} %copy-done.1), kind=kLoop, calls=%fused_computation.23 | loop fusion | flops 524288 | bytes 4194308 | tf_op jit(solution)/shard_map/broadcast_in_dim | solution.py:96
  (2 shorter events, 0.1 us)
Async XLA Ops:
  7.2 102.0 %all-reduce.2.cloned.1.call-start = ((), (), s32[]{:S(2)}) async-start(), calls=%async_computation | async-start | bytes 2097152 | tf_op jit(solution)/shard_map/psum | solution.py:91
  8.6 10.5 %collective-permute-start = (f32[32,2048]{1,0:T(8,128)S(1)}, f32[32,2048]{1,0:T(8,128)S(1)}, u32[]{:S(2)}, u32[]{:S(2)}) collective-permute-start(f32[32,2048]{1,0:T(8,128)S(1)} %get-tuple-element.12), channel_id=1, source_target_pairs={{0,2},{2,4},{4,6},{1,3},{3,5},{5,7},{8,10},{10,12},{12,14},{9,11},... | collective-permute-start | bytes 786440 | tf_op jit(solution)/shard_map/ppermute | solution.py:20
  13.6 9.7 %collective-permute-start.1 = (f32[32,2048]{1,0:T(8,128)S(1)}, f32[32,2048]{1,0:T(8,128)S(1)}, u32[]{:S(2)}, u32[]{:S(2)}) collective-permute-start(f32[32,2048]{1,0:T(8,128)S(1)} %get-tuple-element.13), channel_id=1, source_target_pairs={{2,0},{4,2},{6,4},{3,1},{5,3},{7,5},{10,8},{12,10},{14,12},{11,9},... | collective-permute-start | bytes 786440 | tf_op jit(solution)/shard_map/ppermute | solution.py:22
  23.4 2.8 %collective-permute-start.2 = (f32[192,32]{1,0:T(8,128)S(1)}, f32[192,32]{1,0:T(8,128)S(1)}, u32[]{:S(2)}, u32[]{:S(2)}) collective-permute-start(f32[192,32]{1,0:T(8,128)S(1)} %get-tuple-element.9), channel_id=1, source_target_pairs={{0,1},{2,3},{4,5},{6,7},{8,9},{10,11},{12,13},{14,15},{16,17},{18,... | collective-permute-start | bytes 73736 | tf_op jit(solution)/shard_map/ppermute | solution.py:20
  24.7 10.1 %collective-permute-start.3 = (f32[192,32]{1,0:T(8,128)S(1)}, f32[192,32]{1,0:T(8,128)S(1)}, u32[]{:S(2)}, u32[]{:S(2)}) collective-permute-start(f32[192,32]{1,0:T(8,128)S(1)} %get-tuple-element.8), channel_id=1, source_target_pairs={{1,0},{3,2},{5,4},{7,6},{9,8},{11,10},{13,12},{15,14},{17,16},{19,... | collective-permute-start | bytes 73736 | tf_op jit(solution)/shard_map/ppermute | solution.py:22
  34.8 1.4 copy-start.3
  36.2 6.6 %copy-start.2 = (f32[2]{0:T(128)S(1)}, f32[2]{0:T(128)}, u32[]{:S(2)}) copy-start(f32[2]{0:T(128)} %param.5) | copy-start | bytes 28
  38.0 10.0 %collective-permute-start.4 = (f32[32,2048]{1,0:T(8,128)S(1)}, f32[32,2048]{1,0:T(8,128)S(1)}, u32[]{:S(2)}, u32[]{:S(2)}) collective-permute-start(f32[32,2048]{1,0:T(8,128)S(1)} %get-tuple-element.10), channel_id=1, source_target_pairs={{0,2},{2,4},{4,6},{1,3},{3,5},{5,7},{8,10},{10,12},{12,14},{9,11},... | collective-permute-start | bytes 786440 | tf_op jit(solution)/shard_map/ppermute | solution.py:20
  41.5 11.0 %collective-permute-start.5 = (f32[32,2048]{1,0:T(8,128)S(1)}, f32[32,2048]{1,0:T(8,128)S(1)}, u32[]{:S(2)}, u32[]{:S(2)}) collective-permute-start(f32[32,2048]{1,0:T(8,128)S(1)} %get-tuple-element.11), channel_id=1, source_target_pairs={{2,0},{4,2},{6,4},{3,1},{5,3},{7,5},{10,8},{12,10},{14,12},{11,9},... | collective-permute-start | bytes 786440 | tf_op jit(solution)/shard_map/ppermute | solution.py:22
  52.6 3.5 %collective-permute-start.6 = (f32[192,32]{1,0:T(8,128)S(1)}, f32[192,32]{1,0:T(8,128)S(1)}, u32[]{:S(2)}, u32[]{:S(2)}) collective-permute-start(f32[192,32]{1,0:T(8,128)S(1)} %get-tuple-element.7), channel_id=1, source_target_pairs={{0,1},{2,3},{4,5},{6,7},{8,9},{10,11},{12,13},{14,15},{16,17},{18,... | collective-permute-start | bytes 73736 | tf_op jit(solution)/shard_map/ppermute | solution.py:20
  54.5 10.3 %collective-permute-start.7 = (f32[192,32]{1,0:T(8,128)S(1)}, f32[192,32]{1,0:T(8,128)S(1)}, u32[]{:S(2)}, u32[]{:S(2)}) collective-permute-start(f32[192,32]{1,0:T(8,128)S(1)} %get-tuple-element.6), channel_id=1, source_target_pairs={{1,0},{3,2},{5,4},{7,6},{9,8},{11,10},{13,12},{15,14},{17,16},{19,... | collective-permute-start | bytes 73736 | tf_op jit(solution)/shard_map/ppermute | solution.py:22
  64.7 1.4 %copy-start = (f32[1,128,2048]{2,1,0:T(8,128)S(1)}, f32[1,128,2048]{2,1,0:T(8,128)}, u32[]{:S(2)}) copy-start(f32[1,128,2048]{2,1,0:T(8,128)} %param.4) | copy-start | bytes 3145732
  109.2 19.7 %copy-start.1 = (f32[128,2048]{1,0:T(8,128)S(1)}, f32[128,2048]{1,0:T(8,128)}, u32[]{:S(2)}) copy-start(f32[128,2048]{1,0:T(8,128)} %all-reduce.2.cloned.1.call-done) | copy-start | bytes 3145732
Sparse Core Ops, SparseCore 0:
  69.1 40.0 all-reduce.1
where the time goes:
time: 138 us; the launch traced here: 137 us
  waiting for transfers between devices  55.7 us (40%)
  matrix products  24.5 us (18%)
  starting transfers between devices  17 us (12%)
  blocking collectives  16.8 us (12%)
  between operations  16.4 us (12%)
  other arithmetic  5.45 us (4%)
  local copies, waits for them, and re-layouts  1.48 us (1%)
    psum x1, waiting for transfers between devices, body(): log_mean = lax.psum(weighted, 'hist')  40.2 us
    dot_general x16, matrix products, column_pass(): jnp.dot(window, band_matrix(span_cols), precision=lax.Precision.HIGHEST,...  19.9 us
    psum x1, blocking collectives, body(): total_mass = lax.psum(jnp.sum(mean_field), ('rows', 'cols'))  16.8 us
    ppermute x4, starting transfers between devices, padded_2(): lax.ppermute(tail, axis, [(i, (i + 1) % count) for i in range(ends)])  11.7 us
    ppermute x4, waiting for transfers between devices, padded_2(): lax.ppermute(head, axis, [((i + 1) % count, i) for i in range(ends)])  8.59 us
    ppermute x4, waiting for transfers between devices, padded_2(): lax.ppermute(tail, axis, [(i, (i + 1) % count) for i in range(ends)])  6.85 us
    ppermute x4, starting transfers between devices, padded_2(): lax.ppermute(head, axis, [((i + 1) % count, i) for i in range(ends)])  5.35 us
    dot_general x2, matrix products, row_pass(): jnp.dot(band_matrix(height_out).T, across, precision=lax.Precision.HIGHES...  4.6 us
  transfers between devices with their start and end apart: 9, of which 5 were waited for; matrix products, arithmetic and copies ran while one was open for 14% of the time, Pallas kernels for 0%

commit v1 on v0

v1 whole, which is shorter than its diff:
```python
import functools
import math

import jax
import jax.numpy as jnp
from jax import lax
from jax.experimental import pallas as pl
from jax.experimental.pallas import tpu as pltpu
from jax.sharding import PartitionSpec as P

HALF = 32
SIGMA = 16.0
PIECE = 256
EDGE = 128
MESH = pl.DeviceIdType.MESH
F32 = jnp.float32
BF16 = jnp.bfloat16

TAP_TOTAL = sum(math.exp(-t * t / (2.0 * SIGMA * SIGMA)) for t in range(-HALF, HALF + 1))


def split(x):
    hi = x.astype(BF16)
    lo = (x - hi.astype(F32)).astype(BF16)
    return hi, lo


def dot(a, b):
    return jnp.dot(a, b, preferred_element_type=F32)


def taps(shape, shift):
    a = lax.broadcasted_iota(jnp.int32, shape, 0)
    b = lax.broadcasted_iota(jnp.int32, shape, 1)
    t = (b - a - shift).astype(F32)
    entries = jnp.exp(-t * t / (2.0 * SIGMA * SIGMA)) / TAP_TOTAL
    return jnp.where(jnp.abs(t) <= HALF, entries, 0.0)


def kernel(
    sizes,
    w_ref, v_ref, h_ref,
    mean_ref, diff_ref, scale_ref,
    ev, eh, g1h, g1l, g3h, g3l, r1h, r1l, ch, cl, logs, slots, mass, mslots,
    z_send, z_recv, e_send, e_recv, c_send, c_recv, l_sem, x_send, x_recv, m_send, m_recv,
):
    R, C, H = sizes
    height, width = v_ref.shape
    pieces = width // PIECE
    top = 2 * HALF
    row, col, hist = lax.axis_index("rows"), lax.axis_index("cols"), lax.axis_index("hist")
    flat = row * C + col

    barrier = pltpu.get_barrier_semaphore()
    for k in range(1, R * C):
        other = lax.rem(flat + k, R * C)
        pl.semaphore_signal(
            barrier, inc=1, device_id={"rows": other // C, "cols": lax.rem(other, C)}, device_id_type=MESH
        )
    for k in range(1, H):
        pl.semaphore_signal(barrier, inc=1, device_id={"hist": lax.rem(hist + k, H)}, device_id_type=MESH)

    def own(p):
        cols = pl.ds(pl.multiple_of(p * PIECE, PIECE), PIECE)
        return (
            pltpu.make_async_copy(v_ref.at[:, cols], ev.at[p + 1, pl.ds(top, height)], l_sem.at[0, p]),
            pltpu.make_async_copy(h_ref.at[:, cols], eh.at[p + 1, pl.ds(HALF, height)], l_sem.at[1, p]),
        )

    for p in range(pieces):
        for copy in own(p):
            copy.start()

    pl.semaphore_wait(barrier, R * C - 1 + H - 1)

    def rim(src, dst, depth, edge_rows, send, recv, dev, p, to_up):
        cols = pl.ds(pl.multiple_of(p * PIECE, PIECE), PIECE)
        s = pl.ds(0, depth) if to_up else pl.ds(height - depth, depth)
        d = pl.ds(depth + height, depth) if to_up else pl.ds(0, depth)
        return pltpu.make_async_remote_copy(
            src_ref=src.at[s, cols], dst_ref=dst.at[p + 1, d], send_sem=send, recv_sem=recv,
            device_id=dev, device_id_type=MESH,
        )

    def rims(p, to_up):
        dev = {"rows": row - 1 if to_up else row + 1}
        i = 0 if to_up else 2
        return (
            rim(v_ref, ev, top, None, z_send.at[i, p], z_recv.at[i, p], dev, p, to_up),
            rim(h_ref, eh, HALF, None, z_send.at[i + 1, p], z_recv.at[i + 1, p], dev, p, to_up),
        )

    def side(to_left, up):
        out = []
        scol = pl.ds(0, EDGE) if to_left else pl.ds(width - EDGE, EDGE)
        slot = pieces + 1 if to_left else 0
        dcol = pl.ds(0, EDGE) if to_left else pl.ds(PIECE - EDGE, EDGE)
        dcolumn = col - 1 if to_left else col + 1
        for i, (src, dst, depth) in enumerate(((v_ref, ev, top), (h_ref, eh, HALF))):
            if up == 0:
                s, d = pl.ds(0, height), pl.ds(depth, height)
                dev = {"cols": dcolumn}
                a, b = e_send.at[i, int(to_left)], e_recv.at[i, int(to_left)]
            else:
                s = pl.ds(0, depth) if up < 0 else pl.ds(height - depth, depth)
                d = pl.ds(depth + height, depth) if up < 0 else pl.ds(0, depth)
                dev = {"rows": row + up, "cols": dcolumn}
                n = int(to_left) * 2 + (0 if up < 0 else 1)
                a, b = c_send.at[i, n], c_recv.at[i, n]
            out.append(
                pltpu.make_async_remote_copy(
                    src_ref=src.at[s, scol], dst_ref=dst.at[slot, d, dcol], send_sem=a, recv_sem=b,
                    device_id=dev, device_id_type=MESH,
                )
            )
        return out

    has = {-1: row > 0, 1: row < R - 1}
    has_col = {True: col > 0, False: col < C - 1}

    for up in (-1, 1, 0):
        for to_left in (True, False):
            cond = has_col[to_left]
            if up:
                cond = jnp.logical_and(cond, has[up])

            @pl.when(cond)
            def _():
                for copy in side(to_left, up):
                    copy.start()

    for p in range(pieces):
        for up in (-1, 1):

            @pl.when(has[up])
            def _():
                for copy in rims(p, up < 0):
                    copy.start()

    band = taps(r1h.shape, HALF)
    r1h[...], r1l[...] = split(band)
    for half in range(2):
        rows_in = lax.broadcasted_iota(jnp.int32, (PIECE, PIECE), 0) + half * PIECE
        cols_out = lax.broadcasted_iota(jnp.int32, (PIECE, PIECE), 1)
        t = (rows_in - cols_out - PIECE // 2).astype(F32)
        entries = jnp.exp(-t * t / (2.0 * SIGMA * SIGMA)) / TAP_TOTAL
        ch[half*PIECE:(half+1)*PIECE], cl[half*PIECE:(half+1)*PIECE] = split(jnp.where(jnp.abs(t) <= HALF, entries, 0.0))

    weight_sum = w_ref[0]
    for k in range(1, H):
        weight_sum = weight_sum + w_ref[k]
    own_weight = jnp.full((1, PIECE), w_ref[hist], F32) / jnp.full((1, PIECE), weight_sum, F32)

    def row_ok(rows_count, margin):
        r = lax.broadcasted_iota(jnp.int32, (rows_count, 1), 0) + (row * height - margin)
        return jnp.logical_and(r >= 0, r < R * height)

    def rows_pass(mh, ml, xh, xl):
        return dot(mh[...], xh) + dot(ml[...], xh) + dot(mh[...], xl)

    def scalings_piece(index):
        lanes = lax.broadcasted_iota(jnp.int32, (1, PIECE), 1) + (index - 1) * PIECE
        near = jnp.logical_and(lanes >= -EDGE, lanes < width + EDGE)
        g = lanes + col * width
        ok_cols = jnp.logical_and(near, jnp.logical_and(g >= 0, g < C * width))
        ok = jnp.logical_and(row_ok(height + 2 * top, top), ok_cols)
        f = jnp.where(ok, jnp.exp(ev[index]), 0.0)
        fh, fl = split(f)
        g1h[index], g1l[index] = split(rows_pass(r1h, r1l, fh, fl))

    def cols_pass(ah, al, j):
        xh = jnp.concatenate([ah[j], ah[j + 1]], axis=1)
        xl = jnp.concatenate([al[j], al[j + 1]], axis=1)
        total = dot(xh, ch[...]) + dot(xl, ch[...]) + dot(xh, cl[...])
        return total

    def arrive(conds, make):
        cond = conds[0]
        for c in conds[1:]:
            cond = jnp.logical_and(cond, c)

        @pl.when(cond)
        def _():
            for copy in make():
                copy.wait_recv()

    def wait_side(to_left):
        came = has_col[not to_left]
        arrive((came,), lambda: side(to_left, 0))
        for up in (-1, 1):
            arrive((came, has[-up]), lambda: side(to_left, up))

    wait_side(False)
    scalings_piece(0)

    def x_copy(c, k):
        other = lax.rem(hist + k, H)
        return pltpu.make_async_remote_copy(
            src_ref=slots.at[hist, c], dst_ref=slots.at[hist, c],
            send_sem=x_send.at[k - 1, c], recv_sem=x_recv.at[hist, c],
            device_id={"hist": other}, device_id_type=MESH,
        )

    def step(j, carry):
        @pl.when(j < pieces)
        def _():
            for copy in own(j):
                copy.wait()
            for up in (-1, 1):
                arrive((has[-up],), lambda: rims(j, up < 0))

        @pl.when(j == pieces)
        def _():
            wait_side(True)

        scalings_piece(j + 1)
        smooth_v = cols_pass(g1h, g1l, j)
        masses = jnp.concatenate([eh[j, :, PIECE // 2 :], eh[j + 1, :, : PIECE // 2]], axis=1)
        lanes = lax.broadcasted_iota(jnp.int32, (1, PIECE), 1) + (j * PIECE - PIECE // 2 + col * width)
        ok = jnp.logical_and(
            row_ok(height + top, HALF), jnp.logical_and(lanes >= 0, lanes < C * width)
        )
        ratios = jnp.where(ok, masses / smooth_v, 0.0)
        fill = jnp.zeros((top, PIECE), F32)
        rh, rl = split(jnp.concatenate([ratios, fill], axis=0))
        g3h[j], g3l[j] = split(rows_pass(r1h.at[pl.ds(0, height)], r1l.at[pl.ds(0, height)], rh, rl))

        @pl.when(j >= 1)
        def _():
            c = j - 1
            log_smooth = jnp.log(cols_pass(g3h, g3l, c))
            logs[c] = log_smooth
            slots[hist, c] = own_weight * (ev[c + 1, pl.ds(top, height)] + log_smooth)
            for k in range(1, H):
                x_copy(c, k).start()

        return carry

    for j in range(pieces + 1):
        step(j, 0)

    mass[...] = jnp.zeros_like(mass)

    def combine(c, carry):
        for k in range(1, H):
            source = lax.rem(hist + k, H)
            pltpu.make_async_remote_copy(
                src_ref=slots.at[source, c], dst_ref=slots.at[source, c],
                send_sem=x_send.at[k - 1, c], recv_sem=x_recv.at[source, c],
                device_id={"hist": source}, device_id_type=MESH,
            ).wait_recv()
        log_mean = slots[0, c]
        for k in range(1, H):
            log_mean = log_mean + slots[k, c]
        mean = jnp.exp(log_mean)
        cols = pl.ds(pl.multiple_of(c * PIECE, PIECE), PIECE)
        mean_ref[:, cols] = mean
        diff_ref[:, cols] = log_mean - logs[c]
        part = jnp.sum(mean.reshape(height // 8, 8, PIECE), axis=0)
        mass[...] += part[:, :128] + part[:, 128:]
        return carry

    lax.fori_loop(0, pieces, combine, 0)

    def m_copy(k, index):
        other = lax.rem(flat + k, R * C)
        return pltpu.make_async_remote_copy(
            src_ref=mass, dst_ref=mslots.at[index], send_sem=m_send.at[k - 1], recv_sem=m_recv.at[index],
            device_id={"rows": other // C, "cols": lax.rem(other, C)}, device_id_type=MESH,
        )

    for k in range(1, R * C):
        m_copy(k, flat).start()
    mslots[flat] = mass[...]
    for k in range(1, R * C):
        m_copy(k, lax.rem(flat + k, R * C)).wait_recv()
    total = mslots[0]
    for k in range(1, R * C):
        total = total + mslots[k]
    total = jnp.sum(jnp.sum(total, axis=0, keepdims=True), axis=1, keepdims=True)
    cells = float(height * R * width * C)
    scale_ref[...] = jnp.broadcast_to(cells / total, scale_ref.shape)

    for k in range(1, R * C):
        m_copy(k, flat).wait_send()
    for up in (-1, 1, 0):
        for to_left in (True, False):
            cond = has_col[to_left]
            if up:
                cond = jnp.logical_and(cond, has[up])

            @pl.when(cond)
            def _():
                for copy in side(to_left, up):
                    copy.wait_send()

    def drain(p, carry):
        for up in (-1, 1):

            @pl.when(has[up])
            def _():
                for copy in rims(p, up < 0):
                    copy.wait_send()

        for k in range(1, H):
            x_copy(p, k).wait_send()
        return carry

    lax.fori_loop(0, pieces, drain, 0)


def body(mesh, hists, log_scaling_fields, histogram_weight_list):
    R, C, H = (mesh.shape[a] for a in ("rows", "cols", "hist"))
    masses, fields = hists[0], log_scaling_fields[0]
    height, width = masses.shape
    pieces = width // PIECE
    top = 2 * HALF
    dma = pltpu.SemaphoreType.DMA
    tile = jax.ShapeDtypeStruct((height, width), F32)
    any_spec = pl.BlockSpec(memory_space=pl.ANY)
    vmem = pl.BlockSpec(memory_space=pltpu.VMEM)
    mean, diff, scale = pl.pallas_call(
        functools.partial(kernel, (R, C, H)),
        out_shape=(tile, tile, jax.ShapeDtypeStruct((8, 128), F32)),
        in_specs=[pl.BlockSpec(memory_space=pltpu.SMEM), any_spec, any_spec],
        out_specs=(vmem, vmem, vmem),
        scratch_shapes=[
            pltpu.VMEM((pieces + 2, height + 2 * top, PIECE), F32),
            pltpu.VMEM((pieces + 2, height + top, PIECE), F32),
            pltpu.VMEM((pieces + 2, height + top, PIECE), BF16),
            pltpu.VMEM((pieces + 2, height + top, PIECE), BF16),
            pltpu.VMEM((pieces + 1, height, PIECE), BF16),
            pltpu.VMEM((pieces + 1, height, PIECE), BF16),
            pltpu.VMEM((height + top, height + 2 * top), BF16),
            pltpu.VMEM((height + top, height + 2 * top), BF16),
            pltpu.VMEM((2 * PIECE, PIECE), BF16),
            pltpu.VMEM((2 * PIECE, PIECE), BF16),
            pltpu.VMEM((pieces, height, PIECE), F32),
            pltpu.VMEM((H, pieces, height, PIECE), F32),
            pltpu.VMEM((8, 128), F32),
            pltpu.VMEM((R * C, 8, 128), F32),
            dma((4, pieces)), dma((4, pieces)),
            dma((2, 2)), dma((2, 2)),
            dma((2, 4)), dma((2, 4)),
            dma((2, pieces)),
            dma((max(H - 1, 1), pieces)), dma((H, pieces)),
            dma((max(R * C - 1, 1),)), dma((R * C,)),
        ],
        compiler_params=pltpu.CompilerParams(collective_id=0, has_side_effects=True),
    )(histogram_weight_list, fields, masses)
    factor = scale[0, 0]
    return mean * factor, (diff + jnp.log(factor))[None]


def solution(mesh):
    return jax.shard_map(
        functools.partial(body, mesh),
        mesh=mesh,
        in_specs=(
            P("hist", ("groups", "rows"), "cols"),
            P("hist", ("groups", "rows"), "cols"),
            P(),
        ),
        out_specs=(P(("groups", "rows"), "cols"), P("hist", ("groups", "rows"), "cols")),
        check_vma=False,
    )
```

time: 138 us -> 51.6 us (0.37)
  waiting for transfers between devices: 55.7 us -> 0 us
  Pallas kernels: 0 us -> 44.7 us
  matrix products: 24.5 us -> 0 us
  starting transfers between devices: 17 us -> 0 us
  blocking collectives: 16.8 us -> 0 us
  between operations: 16.4 us -> 1.34 us
    pallas_call x0 -> x1, Pallas kernels: none -> 44.7 us  [body(): pl.pallas_call(functools.partial(kernel, (R, C, H)), out_shape=(tile, til...]
    psum x1 -> x0, waiting for transfers between devices: 40.2 us -> none  [body(): log_mean = lax.psum(weighted, 'hist')]
    dot_general x18 -> x0, matrix products: 24.5 us -> none  [the longest x16 19.9 us: column_pass(): jnp.dot(window, band_matrix(span_cols), precision=lax.Precision.HIGHEST,...]
    ppermute x8 -> x0, starting transfers between devices: 17 us -> none  [the longest x4 11.7 us: padded_2(): lax.ppermute(tail, axis, [(i, (i + 1) % count) for i in range(ends)])]
    psum x1 -> x0, blocking collectives: 16.8 us -> none  [body(): total_mass = lax.psum(jnp.sum(mean_field), ('rows', 'cols'))]
    ppermute x8 -> x0, waiting for transfers between devices: 15.4 us -> none  [the longest x4 8.59 us: padded_2(): lax.ppermute(head, axis, [((i + 1) % count, i) for i in range(ends)])]
    reduce_sum x3 -> x0, other arithmetic: 3.42 us -> none  [the longest x1 2.19 us: body(): total_mass = lax.psum(jnp.sum(mean_field), ('rows', 'cols'))]
    mul x0 -> x1, other arithmetic: none -> 3.02 us  [body(): return (mean * factor, (diff + jnp.log(factor))[None])]
  transfers between devices with their start and end apart: 9 -> 0, of which waited for: 5 -> 0; matrix products, arithmetic and copies ran while one was open for 14% -> 0% of each run, Pallas kernels for 0% -> 0%
where the time goes in v1:
time: 51.6 us; the launch traced here: 51.4 us
  Pallas kernels  44.7 us (87%)
  other arithmetic  4.08 us (8%)
  between operations  1.34 us (3%)
  local copies, waits for them, and re-layouts  1.2 us (2%)
    pallas_call x1, Pallas kernels, body(): pl.pallas_call(functools.partial(kernel, (R, C, H)), out_shape=(tile, til...  44.7 us
    mul x1, other arithmetic, body(): return (mean * factor, (diff + jnp.log(factor))[None])  3.02 us
    slice x1, local copies, waits for them, and re-layouts, body(): factor = scale[0, 0]  1.19 us
    broadcast_in_dim x1, other arithmetic, body(): return (mean * factor, (diff + jnp.log(factor))[None])  1.06 us

profile of v1, /device:TPU:0, one launch (start us, length us, event | category | flops | bytes accessed | tf_op | source)
XLA Modules:
  0.0 51.4 jit_solution(5106218881106510751)
XLA Ops:
  0.6 44.7 %shard_map.50 = (f32[128,2048]{1,0:T(8,128)}, f32[128,2048]{1,0:T(8,128)}, f32[8,128]{1,0:T(8,128)}) custom-call(f32[2]{0:T(128)} %w_ref.1, f32[128,2048]{1,0:T(8,128)} %bitcast.5, f32[128,2048]{1,0:T(8,128)} %bitcast.6), custom_call_target="tpu_custom_call" | custom-call | tf_op jit(solution)/shard_map/pallas_call | solution.py:322
  45.4 1.2 %slice.3 = f32[1,1]{1,0:T(1,128)} slice(f32[8,128]{1,0:T(8,128)} %get-tuple-element.6), slice={[0:1], [0:1]} | slice | bytes 8 | tf_op jit(solution)/shard_map/slice | solution.py:351
  46.6 0.0 copy-start
  46.6 3.0 %broadcast_multiply_fusion = f32[128,2048]{1,0:T(8,128)} fusion(f32[128,2048]{1,0:T(8,128)} %get-tuple-element.5, f32[]{:T(128)} %bitcast.2), kind=kLoop, calls=%fused_computation.1 | loop fusion | flops 262144 | bytes 2097156 | tf_op jit(solution)/shard_map/mul | solution.py:352
  50.3 0.0 copy-done
  50.3 1.1 %add_bitcast_fusion = f32[1,128,2048]{2,1,0:T(8,128)} fusion(f32[128,2048]{1,0:T(8,128)S(1)} %copy-done, f32[]{:T(128)S(6)} %log.3), kind=kLoop, calls=%fused_computation | loop fusion | flops 262144 | bytes 2097156 | tf_op jit(solution)/shard_map/broadcast_in_dim | solution.py:352
Async XLA Ops:
  46.6 3.7 %copy-start = (f32[128,2048]{1,0:T(8,128)S(1)}, f32[128,2048]{1,0:T(8,128)}, u32[]{:S(2)}) copy-start(f32[128,2048]{1,0:T(8,128)} %get-tuple-element.7) | copy-start | bytes 3145732

commit v2 on v1

--- a/solution.py
+++ b/solution.py
@@ -118,8 +118,8 @@
     has = {-1: row > 0, 1: row < R - 1}
     has_col = {True: col > 0, False: col < C - 1}
 
-    for up in (-1, 1, 0):
-        for to_left in (True, False):
+    def send_sides(to_left):
+        for up in (-1, 1, 0):
             cond = has_col[to_left]
             if up:
                 cond = jnp.logical_and(cond, has[up])
@@ -129,6 +129,7 @@
                 for copy in side(to_left, up):
                     copy.start()
 
+    send_sides(False)
     for p in range(pieces):
         for up in (-1, 1):
 
@@ -136,6 +137,8 @@
             def _():
                 for copy in rims(p, up < 0):
                     copy.start()
+
+    send_sides(True)
 
     band = taps(r1h.shape, HALF)
     r1h[...], r1l[...] = split(band)
@@ -277,9 +280,7 @@
     total = mslots[0]
     for k in range(1, R * C):
         total = total + mslots[k]
-    total = jnp.sum(jnp.sum(total, axis=0, keepdims=True), axis=1, keepdims=True)
-    cells = float(height * R * width * C)
-    scale_ref[...] = jnp.broadcast_to(cells / total, scale_ref.shape)
+    scale_ref[0] = jnp.sum(total)
 
     for k in range(1, R * C):
         m_copy(k, flat).wait_send()
@@ -317,13 +318,13 @@
     top = 2 * HALF
     dma = pltpu.SemaphoreType.DMA
     tile = jax.ShapeDtypeStruct((height, width), F32)
-    any_spec = pl.BlockSpec(memory_space=pl.ANY)
+    any_spec = pl.BlockSpec(memory_space=pltpu.HBM)
     vmem = pl.BlockSpec(memory_space=pltpu.VMEM)
     mean, diff, scale = pl.pallas_call(
         functools.partial(kernel, (R, C, H)),
-        out_shape=(tile, tile, jax.ShapeDtypeStruct((8, 128), F32)),
+        out_shape=(tile, tile, jax.ShapeDtypeStruct((1,), F32)),
         in_specs=[pl.BlockSpec(memory_space=pltpu.SMEM), any_spec, any_spec],
-        out_specs=(vmem, vmem, vmem),
+        out_specs=(vmem, vmem, pl.BlockSpec(memory_space=pltpu.SMEM)),
         scratch_shapes=[
             pltpu.VMEM((pieces + 2, height + 2 * top, PIECE), F32),
             pltpu.VMEM((pieces + 2, height + top, PIECE), F32),
@@ -346,9 +347,9 @@
             dma((max(H - 1, 1), pieces)), dma((H, pieces)),
             dma((max(R * C - 1, 1),)), dma((R * C,)),
         ],
-        compiler_params=pltpu.CompilerParams(collective_id=0, has_side_effects=True),
+        compiler_params=pltpu.CompilerParams(collective_id=0, has_side_effects=True, vmem_limit_bytes=(24 + 2 * H) << 20),
     )(histogram_weight_list, fields, masses)
-    factor = scale[0, 0]
+    factor = float(height * R * width * C) / scale[0]
     return mean * factor, (diff + jnp.log(factor))[None]
 
 

time: 51.6 us -> 49.7 us (0.963)
  other arithmetic: 4.08 us -> 2.12 us
  local copies, waits for them, and re-layouts: 1.2 us -> 3.1 us
  Pallas kernels: 44.7 us -> 43 us
    unnamed x2 -> x6, local copies, waits for them, and re-layouts: 0.01 us -> 3.1 us
    mul x1, other arithmetic: 3.02 us -> 1.06 us  [body(): return (mean * factor, (diff + jnp.log(factor))[None])]
    pallas_call x1, Pallas kernels: 44.7 us -> 43 us  [body(): pl.pallas_call(functools.partial(kernel, (R, C, H)), out_shape=(tile, til...]
    slice x1 -> x0, local copies, waits for them, and re-layouts: 1.19 us -> none  [body(): factor = scale[0, 0]]
where the time goes in v2:
time: 49.7 us; the launch traced here: 49.5 us
  Pallas kernels  43 us (87%)
  local copies, waits for them, and re-layouts  3.1 us (6%)
  other arithmetic  2.12 us (4%)
  between operations  1.34 us (3%)
    pallas_call x1, Pallas kernels, body(): pl.pallas_call(functools.partial(kernel, (R, C, H)), out_shape=(tile, til...  43 us
    unnamed x6, local copies, waits for them, and re-layouts  3.1 us
    mul x1, other arithmetic, body(): return (mean * factor, (diff + jnp.log(factor))[None])  1.06 us
    broadcast_in_dim x1, other arithmetic, body(): return (mean * factor, (diff + jnp.log(factor))[None])  1.06 us

profile of v2, /device:TPU:0, one launch (start us, length us, event | category | flops | bytes accessed | tf_op | source)
XLA Modules:
  0.0 49.5 jit_solution(11996272838629819846)
XLA Ops:
  0.6 0.0 copy-start.2
  0.6 0.6 %copy-done.2 = f32[2]{0:T(128)S(1)} copy-done((f32[2]{0:T(128)S(1)}, f32[2]{0:T(128)}, u32[]{:S(2)}) %copy-start.2) | copy-done | bytes 32
  1.3 0.0 copy-start
  1.3 1.2 %copy-done = f32[1,128,2048]{2,1,0:T(8,128)S(1)} copy-done((f32[1,128,2048]{2,1,0:T(8,128)S(1)}, f32[1,128,2048]{2,1,0:T(8,128)}, u32[]{:S(2)}) %copy-start) | copy-done | bytes 1048600
  2.5 0.0 copy-start.1
  2.5 1.2 %copy-done.1 = f32[1,128,2048]{2,1,0:T(8,128)S(1)} copy-done((f32[1,128,2048]{2,1,0:T(8,128)S(1)}, f32[1,128,2048]{2,1,0:T(8,128)}, u32[]{:S(2)}) %copy-start.1) | copy-done | bytes 1048600
  3.7 43.0 %shard_map.50 = (f32[128,2048]{1,0:T(8,128)S(1)}, f32[128,2048]{1,0:T(8,128)S(1)}, f32[1]{0:T(128)}) custom-call(f32[2]{0:T(128)S(1)} %copy-done.2, f32[128,2048]{1,0:T(8,128)S(1)} %bitcast.5, f32[128,2048]{1,0:T(8,128)S(1)} %bitcast.6), custom_call_target="tpu_custom_call" | custom-call | tf_op jit(solution)/shard_map/pallas_call | solution.py:323
  47.3 1.1 %broadcast_multiply_fusion = f32[128,2048]{1,0:T(8,128)} fusion(f32[128,2048]{1,0:T(8,128)S(1)} %get-tuple-element.5, f32[]{:T(128)} %bitcast.2), kind=kLoop, calls=%fused_computation.1 | loop fusion | flops 262144 | bytes 2097156 | tf_op jit(solution)/shard_map/mul | solution.py:353
  48.5 1.1 %add_bitcast_fusion = f32[1,128,2048]{2,1,0:T(8,128)} fusion(f32[128,2048]{1,0:T(8,128)S(1)} %get-tuple-element.7, f32[]{:T(128)S(6)} %log.3), kind=kLoop, calls=%fused_computation | loop fusion | flops 262144 | bytes 2097156 | tf_op jit(solution)/shard_map/broadcast_in_dim | solution.py:353
Async XLA Ops:
  0.6 0.7 %copy-start.2 = (f32[2]{0:T(128)S(1)}, f32[2]{0:T(128)}, u32[]{:S(2)}) copy-start(f32[2]{0:T(128)} %w_ref.1) | copy-start | bytes 28
  1.3 1.2 %copy-start = (f32[1,128,2048]{2,1,0:T(8,128)S(1)}, f32[1,128,2048]{2,1,0:T(8,128)}, u32[]{:S(2)}) copy-start(f32[1,128,2048]{2,1,0:T(8,128)} %param.4) | copy-start | bytes 3145732
  2.5 1.2 %copy-start.1 = (f32[1,128,2048]{2,1,0:T(8,128)S(1)}, f32[1,128,2048]{2,1,0:T(8,128)}, u32[]{:S(2)}) copy-start(f32[1,128,2048]{2,1,0:T(8,128)} %param.3) | copy-start | bytes 3145732

commit v3 on v2

--- a/solution.py
+++ b/solution.py
@@ -347,7 +347,7 @@
             dma((max(H - 1, 1), pieces)), dma((H, pieces)),
             dma((max(R * C - 1, 1),)), dma((R * C,)),
         ],
-        compiler_params=pltpu.CompilerParams(collective_id=0, has_side_effects=True, vmem_limit_bytes=(24 + 2 * H) << 20),
+        compiler_params=pltpu.CompilerParams(collective_id=0, has_side_effects=True, vmem_limit_bytes=51 << 20),
     )(histogram_weight_list, fields, masses)
     factor = float(height * R * width * C) / scale[0]
     return mean * factor, (diff + jnp.log(factor))[None]

time: 49.7 us -> 47.5 us (0.956)
  local copies, waits for them, and re-layouts: 3.1 us -> 0.65 us
    unnamed x6 -> x2, local copies, waits for them, and re-layouts: 3.1 us -> 0.65 us
where the time goes in v3:
time: 47.5 us; the launch traced here: 47.3 us
  Pallas kernels  43.2 us (91%)
  other arithmetic  2.12 us (4%)
  between operations  1.37 us (3%)
  local copies, waits for them, and re-layouts  0.65 us (1%)
    pallas_call x1, Pallas kernels, body(): pl.pallas_call(functools.partial(kernel, (R, C, H)), out_shape=(tile, til...  43.2 us
    mul x1, other arithmetic, body(): return (mean * factor, (diff + jnp.log(factor))[None])  1.06 us
    broadcast_in_dim x1, other arithmetic, body(): return (mean * factor, (diff + jnp.log(factor))[None])  1.06 us

profile of v3, /device:TPU:0, one launch (start us, length us, event | category | flops | bytes accessed | tf_op | source)
XLA Modules:
  0.0 47.3 jit_solution(9255218423134476632)
XLA Ops:
  0.6 0.0 copy-start
  0.6 0.6 %copy-done = f32[2]{0:T(128)S(1)} copy-done((f32[2]{0:T(128)S(1)}, f32[2]{0:T(128)}, u32[]{:S(2)}) %copy-start) | copy-done | bytes 32
  1.3 43.2 %shard_map.50 = (f32[128,2048]{1,0:T(8,128)S(1)}, f32[128,2048]{1,0:T(8,128)S(1)}, f32[1]{0:T(128)}) custom-call(f32[2]{0:T(128)S(1)} %copy-done, f32[128,2048]{1,0:T(8,128)} %bitcast.5, f32[128,2048]{1,0:T(8,128)} %bitcast.6), custom_call_target="tpu_custom_call" | custom-call | tf_op jit(solution)/shard_map/pallas_call | solution.py:323
  45.1 1.1 %broadcast_multiply_fusion = f32[128,2048]{1,0:T(8,128)} fusion(f32[128,2048]{1,0:T(8,128)S(1)} %get-tuple-element.5, f32[]{:T(128)} %bitcast.2), kind=kLoop, calls=%fused_computation.1 | loop fusion | flops 262144 | bytes 2097156 | tf_op jit(solution)/shard_map/mul | solution.py:353
  46.2 1.1 %add_bitcast_fusion = f32[1,128,2048]{2,1,0:T(8,128)} fusion(f32[128,2048]{1,0:T(8,128)S(1)} %get-tuple-element.7, f32[]{:T(128)S(6)} %log.3), kind=kLoop, calls=%fused_computation | loop fusion | flops 262144 | bytes 2097156 | tf_op jit(solution)/shard_map/broadcast_in_dim | solution.py:353
Async XLA Ops:
  0.6 0.7 %copy-start = (f32[2]{0:T(128)S(1)}, f32[2]{0:T(128)}, u32[]{:S(2)}) copy-start(f32[2]{0:T(128)} %w_ref.1) | copy-start | bytes 28
